TPU v7x, 32 devices: a whole 2x2x4 slice. The times are simulated.
32 devices in a mesh: group: 8 (over z, core), dp: 4 (over y, x).
Axes of the slice: x: 2, y: 2, z: 4, core: 2. Of those that a mesh axis runs over, the one named last changes fastest.
Arguments:
- resp_q: bfloat16 [8, 1024, 4096], P('group', 'dp'), may hold values from -410 to 410
- resp_k: bfloat16 [8, 1024, 4096], P('group', 'dp'), may hold values from -410 to 410
- resp_v: bfloat16 [8, 1024, 4096], P('group', 'dp'), may hold values from -6 to 6
- prompt_k: bfloat16 [8, 512, 4096], P('group', 'dp'), may hold values from -410 to 410
- prompt_v: bfloat16 [8, 512, 4096], P('group', 'dp'), may hold values from -6 to 6
- prompt_len: int32 [8], P('group'), may hold values from 128 to 512
- resp_len: int32 [8, 4], P('group', 'dp'), may hold values from 1 to 256, as said below
- assign: int32 [8, 8], P('group', 'dp'), may hold values from 0 to 15, as said below
- rewards: float32 [8, 4], P('group', 'dp'), may hold values from -18 to 18
- feat_q: bfloat16 [32, 128, 128], replicated, may hold values from -1 to 1
- feat_k: bfloat16 [32, 128, 128], replicated, may hold values from -1 to 1
Outputs:
- attn_out: bfloat16 [8, 512, 4096], P('group', 'dp')
- token_adv: float32 [8, 512], P('group', 'dp')
Inputs may be any that keep to these rules, and one draw needn't show every extreme that they name: Response r of a prompt has ceil(resp_len / 64) live blocks; these counts sum to 2 * 4 over a prompt's responses, and one response of every prompt has 4 blocks. `assign`: entry d * 2 + j names the block r * 4 + c (block c of response r) whose outputs go to slot j of device d of dp. Every live block of the prompt is named exactly once, and the 2 slots of one device name blocks of different responses.
All inputs are finite; a program needn't handle non-finite values.
Results may differ from a plain program's by a relative error of at most 0.0085.
Values may be sent and summed in bfloat16 or wider, within the bound.
A program may use at most 128 MiB of HBM per device.

v0:
```python
import jax
import jax.numpy as jnp
from jax import lax
from jax.sharding import PartitionSpec as P

BLK = 64


def features(rows, weights):
    logits = jnp.einsum("thd,hdf->thf", rows, weights, preferred_element_type=jnp.float32)
    return jnp.concatenate(
        [jax.nn.softmax(logits, axis=-1), jax.nn.softmax(-logits, axis=-1)], axis=-1
    ).astype(jnp.bfloat16)


def state_terms(query_feat, state_rounded, total_rounded):
    numerator = jnp.einsum(
        "thf,hfe->the", query_feat, state_rounded, preferred_element_type=jnp.float32
    )
    denominator = jnp.einsum(
        "thf,hf->th", query_feat, total_rounded, preferred_element_type=jnp.float32
    )
    return (numerator.astype(jnp.bfloat16), denominator.astype(jnp.bfloat16))


def body(
    resp_q,
    resp_k,
    resp_v,
    prompt_k,
    prompt_v,
    prompt_len,
    resp_len,
    assign,
    rewards,
    feat_q,
    feat_k,
):
    dp_count = lax.axis_size("dp")
    my_index = lax.axis_index("dp")
    head_count = feat_q.shape[0]
    head_width = feat_q.shape[1]
    length = resp_q.shape[1]
    prompt_rows = prompt_k.shape[1]
    queries = resp_q[0].reshape(length, head_count, head_width)
    key_rows = resp_k[0].reshape(length, head_count, head_width)
    values = resp_v[0].reshape(length, head_count, head_width)
    prompt_keys = prompt_k[0].reshape(prompt_rows, head_count, head_width)
    prompt_values = prompt_v[0].reshape(prompt_rows, head_count, head_width)
    keep = my_index * prompt_rows + jnp.arange(prompt_rows) < prompt_len[0]
    prompt_feat = jnp.where(
        keep[:, None, None], features(prompt_keys, feat_k), jnp.zeros((), jnp.bfloat16)
    )
    part_state = jnp.einsum(
        "shf,she->hfe", prompt_feat, prompt_values, preferred_element_type=jnp.float32
    )
    part_total = jnp.sum(prompt_feat.astype(jnp.float32), axis=0)
    query_feat = features(queries, feat_q)
    key_feat = features(key_rows, feat_k)
    kv_share, total_share = (
        lax.psum_scatter(part_state, "dp", scatter_dimension=0, tiled=True),
        lax.psum_scatter(part_total, "dp", scatter_dimension=0, tiled=True),
    )
    kv_state, key_total = (
        lax.all_gather(kv_share.astype(jnp.bfloat16), "dp", axis=0, tiled=True),
        lax.all_gather(total_share.astype(jnp.bfloat16), "dp", axis=0, tiled=True),
    )
    prompt_num, prompt_den = state_terms(query_feat, kv_state, key_total)
    causal = jnp.arange(length)[:, None] >= jnp.arange(length)[None, :]
    scores = jnp.einsum("thf,shf->hts", query_feat, key_feat, preferred_element_type=jnp.float32)
    scores = jnp.where(causal[None], scores, jnp.float32(0.0))
    intra_den = jnp.sum(scores, axis=-1)
    intra_num = jnp.einsum(
        "hts,she->the", scores.astype(jnp.bfloat16), values, preferred_element_type=jnp.float32
    )
    combined = (prompt_num.astype(jnp.float32) + intra_num) / (
        prompt_den.astype(jnp.float32) + intra_den.T
    )[:, :, None]
    live_rows = jnp.arange(length) < resp_len[0, 0]
    combined = jnp.where(live_rows[:, None, None], combined, jnp.float32(0.0))
    result = combined.astype(jnp.bfloat16).reshape(-1, BLK, head_count * head_width)
    pieces = result.shape[0]
    slot_width = assign.shape[1]
    table, lengths = (
        lax.all_gather(assign, "dp", axis=1, tiled=True),
        lax.all_gather(resp_len, "dp", axis=1, tiled=True),
    )
    slot_ids = table[0].reshape(dp_count, slot_width)
    own_ids = assign[0]
    source = own_ids // pieces
    stretch_index = own_ids % pieces
    picker = source[:, None] == jnp.arange(dp_count)[None, :]
    mine_mask = jnp.any(
        slot_ids[:, :, None] == my_index * pieces + jnp.arange(pieces)[None, None, :], axis=1
    )
    outgoing = jnp.einsum(
        "dc,cbe->dbe", mine_mask.astype(jnp.bfloat16), result, preferred_element_type=jnp.float32
    ).astype(jnp.bfloat16)
    incoming = lax.all_to_all(outgoing, "dp", split_axis=0, concat_axis=0, tiled=True)
    attended = jnp.einsum(
        "jd,dbe->jbe", picker.astype(jnp.bfloat16), incoming, preferred_element_type=jnp.float32
    ).astype(jnp.bfloat16)
    attended = attended.reshape(1, slot_width * BLK, head_count * head_width)
    reward_all = lax.all_gather(rewards, "dp", axis=1, tiled=True)[0]
    centred = reward_all - jnp.sum(reward_all) / dp_count
    spread = lax.psum(jnp.sum(centred * centred), "group")
    advantage = centred / jnp.sqrt(spread / (lax.axis_size("group") * dp_count) + 1e-06)
    slot_adv = jnp.sum(jnp.where(picker, advantage[None, :], jnp.float32(0.0)), axis=1)
    slot_len = jnp.sum(jnp.where(picker, lengths[0][None, :], 0), axis=1)
    positions = stretch_index[:, None] * BLK + jnp.arange(BLK)[None, :]
    token_adv = jnp.where(positions < slot_len[:, None], slot_adv[:, None], jnp.float32(0.0))
    return (attended, token_adv.reshape(1, slot_width * BLK))


def solution(mesh):
    return jax.shard_map(
        body,
        mesh=mesh,
        in_specs=(
            P("group", "dp", None),
            P("group", "dp", None),
            P("group", "dp", None),
            P("group", "dp", None),
            P("group", "dp", None),
            P("group"),
            P("group", "dp"),
            P("group", "dp"),
            P("group", "dp"),
            P(),
            P(),
        ),
        out_specs=(P("group", "dp", None), P("group", "dp")),
        check_vma=False,
    )
```

profile of v0, /device:TPU:0, one launch (start us, length us, event | category | flops | bytes accessed | tf_op | source)
XLA Modules:
  0.0 187.2 jit_solution(10308482313674577774)
XLA Ops:
  8.8 2.5 %fusion.63 = (f32[128,32]{0,1:T(8,128)S(1)}, f32[128,32,128]{0,2,1:T(8,128)}) fusion(bf16[32,128,128]{2,1,0:T(8,128)(2,1)S(1)} %copy-done, bf16[128,32,128]{2,1,0:T(8,128)(2,1)S(1)} %bitcast.135), kind=kOutput, calls=%fused_computation.102 | convolution fusion | flops 135790720 | bytes 4210688 | tf_op jit(solution)/shard_map/sub | solution.py:12
  14.7 2.4 %copy.92 = bf16[16,8,32,128]{3,2,1,0:T(8,128)(2,1)} copy(bf16[16,8,32,128]{3,1,2,0:T(8,128)(2,1)} %bitcast.142) | data formatting | bytes 2097152
  20.8 2.8 %fusion.38 = f32[32,256,128]{2,1,0:T(8,128)} fusion(bf16[128,32,128]{0,2,1:T(8,128)(2,1)S(1)} %get-tuple-element.29, bf16[128,32,128]{0,2,1:T(8,128)(2,1)S(1)} %get-tuple-element.30, pred[128]{0:T(512)(128)(4,1)S(1)} %add_compare_fusion, bf16[128,32,128]{2,1,0:T(8,128)(2,1)S(1)} %bitcast.143), kind=kOutput, calls=%fused_computation.58 | convolution fusion | flops 273678336 | bytes 7340160 | tf_op jit(solution)/shard_map/shf,she->hfe/dot_general | solution.py:54
  26.1 8.9 %all-reduce.4 = (s32[8]{0:T(128)S(1)}, s32[4]{0:T(128)S(1)}) all-reduce(s32[8]{0:T(128)S(1)} %get-tuple-element.8, s32[4]{0:T(128)S(1)} %bitcast_dynamic-update-slice_fusion.1), channel_id=1, replica_groups=mesh['group'=8,'dp'=4] {'dp'}, use_global_device_ids=true, to_apply=%add | all-reduce | flops 12 | bytes 96
  37.2 3.4 %copy.93 = bf16[32,8,32,128]{3,2,1,0:T(8,128)(2,1)} copy(bf16[32,8,32,128]{3,1,2,0:T(8,128)(2,1)} %bitcast.138) | data formatting | bytes 4194304
  44.5 2.4 %convert_reduce_fusion = f32[32,256]{1,0:T(8,128)S(1)} fusion(bf16[128,32,128]{0,2,1:T(8,128)(2,1)} %copy-done.4, bf16[128,32,128]{0,2,1:T(8,128)(2,1)} %copy-done.5, pred[128]{0:T(512)(128)(4,1)S(1)} %add_compare_fusion), kind=kLoop, calls=%fused_computation.30 | loop fusion | flops 7331840 | bytes 2130048 | tf_op jit(solution)/shard_map/reduce_sum | solution.py:57
  46.9 16.8 %all-reduce.5 = (bf16[32,256]{1,0:T(8,128)(2,1)S(1)}, f32[4]{0:T(128)S(1)}) all-reduce(f32[32,256]{1,0:T(8,128)S(1)} %convert_reduce_fusion, f32[4]{0:T(128)S(1)} %bitcast_dynamic-update-slice_fusion), channel_id=3, replica_groups=mesh['group'=8,'dp'=4] {'dp'}, use_global_device_ids=true, to_apply=%region_15.16.clone | all-reduce | flops 8196 | bytes 49184
  63.7 8.6 %all_gather.17 = bf16[32,256]{1,0:T(8,128)(2,1)S(1)} all-gather(bf16[8,256]{1,0:T(8,128)(2,1)S(1)} %dynamic-slice_convert_fusion), channel_id=1, replica_groups=mesh['group'=8,'dp'=4] {'dp'}, dimensions={0}, use_global_device_ids=true | all-gather | bytes 20480 | tf_op jit(solution)/shard_map/all_gather | solution.py:66
  72.5 3.2 %fusion.31 = f32[32,128,256]{2,1,0:T(8,128)S(1)} fusion(bf16[32,128,128]{2,1,0:T(8,128)(2,1)} %param.20, bf16[256,32,128]{2,1,0:T(8,128)(2,1)} %bitcast.134), kind=kOutput, calls=%fused_computation.50 | convolution fusion | flops 268435456 | bytes 7340032 | tf_op jit(solution)/shard_map/thd,hdf->thf/dot_general | solution.py:10
  75.7 4.0 %fusion.61 = (f32[256,32]{0,1:T(8,128)S(1)}, f32[256,32,128]{0,2,1:T(8,128)S(1)}) fusion(f32[32,128,256]{2,1,0:T(8,128)S(1)} %fusion.31), kind=kOutput, calls=%fused_computation.100 | output fusion | flops 4194431 | bytes 8421376 | tf_op jit(solution)/shard_map/sub | solution.py:12
  79.7 3.9 %fusion.62 = (f32[256,32]{0,1:T(8,128)S(1)}, f32[256,32,128]{0,2,1:T(8,128)S(1)}) fusion(f32[32,128,256]{2,1,0:T(8,128)S(1)} %fusion.31), kind=kOutput, calls=%fused_computation.101 | output fusion | flops 2097279 | bytes 8421376 | tf_op jit(solution)/shard_map/sub | solution.py:12
  88.9 3.0 %fusion.59 = (f32[256,32]{0,1:T(8,128)S(1)}, f32[256,32,128]{0,2,1:T(8,128)}) fusion(f32[32,128,256]{2,1,0:T(8,128)S(1)} %fusion.29), kind=kOutput, calls=%fused_computation.98 | output fusion | flops 4194431 | bytes 8421376 | tf_op jit(solution)/shard_map/sub | solution.py:12
  94.1 4.4 %fusion.60 = (f32[256,32]{0,1:T(8,128)S(1)}, f32[256,32,128]{0,2,1:T(8,128)S(1)}) fusion(f32[32,128,256]{2,1,0:T(8,128)} %copy-done.2), kind=kOutput, calls=%fused_computation.99 | output fusion | flops 2097279 | bytes 8421376 | tf_op jit(solution)/shard_map/sub | solution.py:12
  98.8 3.2 %divide_convert_fusion = (bf16[256,32,128]{0,2,1:T(8,128)(2,1)}, bf16[256,32,128]{0,2,1:T(8,128)(2,1)}) fusion(f32[256,32,128]{0,2,1:T(8,128)S(1)} %copy-done.3, f32[256,32]{0,1:T(8,128)S(1)} %get-tuple-element.11, f32[256,32,128]{0,2,1:T(8,128)S(1)} %get-tuple-element.14, f32[256,32]{0,1:T(8,128)S(1)} %get-tuple-element.13), kind=kLoop, calls=%fused_computation.32 | loop fusion | flops 4194304 | bytes 12648448 | tf_op jit(solution)/shard_map/convert.2
  102.0 5.3 %select_reduce_fusion = (f32[32,256]{1,0:T(8,128)S(1)}, bf16[32,256,256]{1,2,0:T(8,128)(2,1)}) fusion(pred[256,256]{0,1:T(8,128)(4,1)S(1)} %iota_compare_fusion, bf16[256,32,128]{0,2,1:T(8,128)(2,1)} %get-tuple-element.25, bf16[256,32,128]{0,2,1:T(8,128)(2,1)} %get-tuple-element.26, bf16[256,32,128]{0,2,1:T(8,128)(2,1)S(1)} %copy-done.9, ...), kind=kOutput, calls=%fused_computation.6 | convolution fusion | flops 1096802304 | bytes 12681216 | tf_op jit(solution)/shard_map/thf,shf->hts/dot_general | solution.py:70
  107.3 5.8 %fusion.6 = f32[32,256,128]{1,2,0:T(8,128)} fusion(bf16[32,256,256]{1,2,0:T(8,128)(2,1)} %get-tuple-element.20, pred[256,256]{0,1:T(8,128)(4,1)S(1)} %iota_compare_fusion, bf16[256,32,128]{2,1,0:T(8,128)(2,1)S(1)} %bitcast.140), kind=kOutput, calls=%fused_computation.10 | convolution fusion | flops 538968064 | bytes 10551296 | tf_op jit(solution)/shard_map/hts,she->the/dot_general | solution.py:73
  113.1 16.5 %all-gather.2.cloned.1.call-done = bf16[32,256,128]{2,1,0:T(8,128)(2,1)} async-done(((bf16[8,256,128]{2,1,0:T(8,128)(2,1)}), bf16[32,256,128]{2,1,0:T(8,128)(2,1)}) %all-gather.2.cloned.1.call-update) | async-done | bytes 2097168 | tf_op jit(solution)/shard_map/all_gather | solution.py:65
  129.6 5.1 %fusion.13 = bf16[256,32,128]{0,2,1:T(8,128)(2,1)S(1)} fusion(f32[32,256,128]{1,2,0:T(8,128)} %fusion.6, f32[256,32]{0,1:T(8,128)S(1)} %add_bitcast_fusion, pred[256]{0:T(512)(128)(4,1)S(1)} %iota_compare_fusion.1, bf16[32,256,128]{2,1,0:T(8,128)(2,1)} %all-gather.2.cloned.1.call-done, bf16[256,32,128]{0,2,1:T(8,128)(2,1)} %copy-done.8, ...), kind=kOutput, calls=%fused_computation.19 | convolution fusion | flops 551550976 | bytes 12615936 | tf_op jit(solution)/shard_map/thf,hfe->the/dot_general | solution.py:17
  134.7 3.3 %reshape.185 = bf16[4,64,4096]{1,0,2:T(4,128)(2,1)} reshape(bf16[256,32,128]{0,2,1:T(8,128)(2,1)S(1)} %fusion.13) | data formatting | bytes 4194304 | tf_op jit(solution)/shard_map/reshape | solution.py:81
  138.0 6.6 %copy.74 = bf16[4,64,4096]{2,0,1:T(4,128)(2,1)S(1)} copy(bf16[4,64,4096]{1,0,2:T(4,128)(2,1)} %reshape.185) | data formatting | bytes 4194304 | tf_op jit(solution)/shard_map/reshape | solution.py:81
  145.8 2.5 %copy.75 = bf16[4,64,4096]{2,1,0:T(8,128)(2,1)} copy(bf16[4,64,4096]{2,0,1:T(4,128)(2,1)S(1)} %convolution_convert_fusion) | data formatting | bytes 4194304 | tf_op jit(solution)/shard_map/convert_element_type | solution.py:98
  148.3 3.6 %all-to-all-start = ((bf16[4,64,4096]{2,1,0:T(8,128)(2,1)}), bf16[4,64,4096]{2,1,0:T(8,128)(2,1)S(1)}, u32[]{:S(2)}, u32[]{:S(2)}) async-start(bf16[4,64,4096]{2,1,0:T(8,128)(2,1)} %copy.75), calls=%async_computation.1 | async-start | bytes 4194304 | tf_op jit(solution)/shard_map/all_to_all | solution.py:99
  153.8 16.8 %psum.7 = f32[]{:T(128)} all-reduce(f32[]{:T(128)} %multiply_reduce_fusion), channel_id=1, replica_groups=mesh['group'=8,'dp'=4] {'group'}, use_global_device_ids=true, to_apply=%region_20.21 | all-reduce | flops 1 | bytes 8 | tf_op jit(solution)/shard_map/psum | solution.py:106
  172.4 4.5 %all-to-all-done = bf16[4,64,4096]{2,1,0:T(8,128)(2,1)S(1)} async-done(((bf16[4,64,4096]{2,1,0:T(8,128)(2,1)}), bf16[4,64,4096]{2,1,0:T(8,128)(2,1)S(1)}, u32[]{:S(2)}, u32[]{:S(2)}) %all-to-all-start) | async-done | bytes 2097184 | tf_op jit(solution)/shard_map/all_to_all | solution.py:99
  (71 shorter events, 28.7 us)
Async XLA Ops:
  7.2 1.6 copy-start
  7.2 84.8 %reduce-scatter.2.cloned.1.call-start = ((), (), s32[]{:S(2)}) async-start(), calls=%async_computation.2 | async-start | bytes 5242880 | tf_op jit(solution)/shard_map/reduce_scatter | solution.py:61
  17.1 3.6 %copy-start.12 = (bf16[16,8,32,128]{3,2,1,0:T(8,128)(2,1)S(1)}, bf16[16,8,32,128]{3,2,1,0:T(8,128)(2,1)}, u32[]{:S(2)}) copy-start(bf16[16,8,32,128]{3,2,1,0:T(8,128)(2,1)} %copy.92) | copy-start | bytes 3145732
  19.4 1.0 copy-start.4
  19.4 1.3 copy-start.5
  20.8 3.5 %copy-start.13 = (u32[32]{0:T(128)S(1)}, u32[32]{0:T(128)}, u32[]{:S(2)}) copy-start(u32[32]{0:T(128)} %constant.66) | copy-start | bytes 388
  20.8 5.2 %copy-start.14 = (s32[1,2]{1,0:T(1,128)S(1)}, s32[1,2]{1,0:T(1,128)}, u32[]{:S(2)}) copy-start(s32[1,2]{1,0:T(1,128)} %param.18) | copy-start | bytes 28
  23.5 106.1 %all-gather.2.cloned.1.call-start = ((), (), s32[]{:S(2)}) async-start(), calls=%async_computation.3 | async-start | bytes 2621440 | tf_op jit(solution)/shard_map/all_gather | solution.py:65
  35.0 5.7 %copy-start.6 = (bf16[1,256,4096]{2,1,0:T(8,128)(2,1)S(1)}, bf16[1,256,4096]{2,1,0:T(8,128)(2,1)}, u32[]{:S(2)}) copy-start(bf16[1,256,4096]{2,1,0:T(8,128)(2,1)} %param.13) | copy-start | bytes 6291460
  84.9 2.0 %copy-start.8 = (bf16[256,32,128]{0,2,1:T(8,128)(2,1)}, bf16[256,32,128]{0,2,1:T(8,128)(2,1)S(1)}, u32[]{:S(2)}) copy-start(bf16[256,32,128]{0,2,1:T(8,128)(2,1)S(1)} %get-tuple-element.27) | copy-start | bytes 6291460
  84.9 2.0 %copy-start.10 = (bf16[256,32,128]{0,2,1:T(8,128)(2,1)}, bf16[256,32,128]{0,2,1:T(8,128)(2,1)S(1)}, u32[]{:S(2)}) copy-start(bf16[256,32,128]{0,2,1:T(8,128)(2,1)S(1)} %get-tuple-element.28) | copy-start | bytes 6291460
  86.9 2.0 %copy-start.2 = (f32[32,128,256]{2,1,0:T(8,128)}, f32[32,128,256]{2,1,0:T(8,128)S(1)}, u32[]{:S(2)}) copy-start(f32[32,128,256]{2,1,0:T(8,128)S(1)} %fusion.29) | copy-start | bytes 12582916
  94.1 4.6 %copy-start.3 = (f32[256,32,128]{0,2,1:T(8,128)S(1)}, f32[256,32,128]{0,2,1:T(8,128)}, u32[]{:S(2)}) copy-start(f32[256,32,128]{0,2,1:T(8,128)} %get-tuple-element.12) | copy-start | bytes 12582916
  98.8 3.2 %copy-start.9 = (bf16[256,32,128]{0,2,1:T(8,128)(2,1)S(1)}, bf16[256,32,128]{0,2,1:T(8,128)(2,1)}, u32[]{:S(2)}) copy-start(bf16[256,32,128]{0,2,1:T(8,128)(2,1)} %copy-done.8) | copy-start | bytes 6291460
  98.8 3.2 %copy-start.11 = (bf16[256,32,128]{0,2,1:T(8,128)(2,1)S(1)}, bf16[256,32,128]{0,2,1:T(8,128)(2,1)}, u32[]{:S(2)}) copy-start(bf16[256,32,128]{0,2,1:T(8,128)(2,1)} %copy-done.10) | copy-start | bytes 6291460
  102.0 5.3 %copy-start.7 = (bf16[32,8,32,128]{3,2,1,0:T(8,128)(2,1)S(1)}, bf16[32,8,32,128]{3,2,1,0:T(8,128)(2,1)}, u32[]{:S(2)}) copy-start(bf16[32,8,32,128]{3,2,1,0:T(8,128)(2,1)} %copy.95) | copy-start | bytes 6291460
  148.3 28.6 %all-to-all-start = ((bf16[4,64,4096]{2,1,0:T(8,128)(2,1)}), bf16[4,64,4096]{2,1,0:T(8,128)(2,1)S(1)}, u32[]{:S(2)}, u32[]{:S(2)}) async-start(bf16[4,64,4096]{2,1,0:T(8,128)(2,1)} %copy.75), calls=%async_computation.1 | async-start | bytes 4194304 | tf_op jit(solution)/shard_map/all_to_all | solution.py:99
  152.0 28.4 %copy-start.1 = (bf16[32,128,128]{2,1,0:T(8,128)(2,1)S(1)}, bf16[32,128,128]{2,1,0:T(8,128)(2,1)}, u32[]{:S(2)}) copy-start(bf16[32,128,128]{2,1,0:T(8,128)(2,1)} %param.21) | copy-start | bytes 3145732
Sparse Core Ops, SparseCore 0:
  23.7 56.5 reduce-scatter.1
  94.2 35.3 all-gather.1
where the time goes:
time: 188 us; the launch traced here: 187 us
  blocking collectives  51.1 us (27%)
  local copies, waits for them, and re-layouts  31.5 us (17%)
  matrix products  30.7 us (16%)
  other arithmetic  30.3 us (16%)
  waiting for transfers between devices  21.1 us (11%)
  between operations  18.8 us (10%)
  starting transfers between devices  3.69 us (2%)
    unnamed x2, blocking collectives  25.6 us
    psum x1, blocking collectives, body(): spread = lax.psum(jnp.sum(centred * centred), 'group')  16.8 us
    unnamed x41, local copies, waits for them, and re-layouts  16.8 us
    all_gather x1, waiting for transfers between devices, body(): lax.all_gather(kv_share.astype(jnp.bfloat16), 'dp', axis=0, tiled=True)  16.5 us
    sub x3, other arithmetic, features(): jax.nn.softmax(logits, axis=-1)  10.2 us
    reshape x2, local copies, waits for them, and re-layouts, body(): combined.astype(jnp.bfloat16).reshape(-1, BLK, head_count * head_width)  9.89 us
    all_gather x1, blocking collectives, body(): lax.all_gather(total_share.astype(jnp.bfloat16), 'dp', axis=0, tiled=True)  8.64 us
    sub x2, other arithmetic, features(): jax.nn.softmax(-logits, axis=-1)  7.03 us
  transfers between devices with their start and end apart: 3, of which 2 were waited for; matrix products, arithmetic and copies ran while one was open for 27% of the time, Pallas kernels for 0%

commit v1 on v0

--- a/solution.py
+++ b/solution.py
@@ -4,6 +4,12 @@
 from jax.sharding import PartitionSpec as P
 
 BLK = 64
+
+
+def step_on_frames(sheet, array_axis):
+    high = jnp.stack([sheet] * jax.lax.axis_size("dp"))
+    x_new = jax.lax.all_to_all(high, split_axis=0, axis_name="dp", concat_axis=0)
+    return jnp.concatenate(x_new, axis=array_axis)
 
 
 def features(rows, weights):
@@ -62,7 +68,7 @@
         lax.psum_scatter(part_total, "dp", scatter_dimension=0, tiled=True),
     )
     kv_state, key_total = (
-        lax.all_gather(kv_share.astype(jnp.bfloat16), "dp", axis=0, tiled=True),
+        step_on_frames(kv_share.astype(jnp.bfloat16), 0),
         lax.all_gather(total_share.astype(jnp.bfloat16), "dp", axis=0, tiled=True),
     )
     prompt_num, prompt_den = state_terms(query_feat, kv_state, key_total)

time: 188 us -> 181 us (0.963)
  waiting for transfers between devices: 21.1 us -> 9.08 us
  starting transfers between devices: 3.69 us -> 7.47 us
  matrix products: 30.7 us -> 32.6 us
  blocking collectives: 51.1 us -> 49.2 us
    all_gather x1 -> x0, waiting for transfers between devices: 16.5 us -> none  [body(): lax.all_gather(kv_share.astype(jnp.bfloat16), 'dp', axis=0, tiled=True)]
    all_to_all x0 -> x1, waiting for transfers between devices: none -> 4.64 us  [step_on_frames(): jax.lax.all_to_all(high, split_axis=0, axis_name='dp', concat_axis=0)]
    all_to_all x0 -> x1, starting transfers between devices: none -> 3.83 us  [step_on_frames(): jax.lax.all_to_all(high, split_axis=0, axis_name='dp', concat_axis=0)]
    dot_general x1, matrix products: 5.31 us -> 7.41 us  [body(): jnp.einsum('thf,shf->hts', query_feat, key_feat, preferred_element_type=j...]
    psum x1, blocking collectives: 16.8 us -> 14.8 us  [body(): spread = lax.psum(jnp.sum(centred * centred), 'group')]
    unnamed x41 -> x35, local copies, waits for them, and re-layouts: 16.8 us -> 16.3 us
  transfers between devices with their start and end apart: 3 -> 3, of which waited for: 2 -> 2; matrix products, arithmetic and copies ran while one was open for 27% -> 30% of each run, Pallas kernels for 0% -> 0%
where the time goes in v1:
time: 181 us; the launch traced here: 180 us
  blocking collectives  49.2 us (27%)
  local copies, waits for them, and re-layouts  32.6 us (18%)
  matrix products  32.6 us (18%)
  other arithmetic  29.9 us (17%)
  between operations  19 us (10%)
  waiting for transfers between devices  9.08 us (5%)
  starting transfers between devices  7.47 us (4%)
    unnamed x2, blocking collectives  25.6 us
    unnamed x35, local copies, waits for them, and re-layouts  16.3 us
    psum x1, blocking collectives, body(): spread = lax.psum(jnp.sum(centred * centred), 'group')  14.8 us
    sub x3, other arithmetic, features(): jax.nn.softmax(logits, axis=-1)  9.75 us
    reshape x2, local copies, waits for them, and re-layouts, body(): combined.astype(jnp.bfloat16).reshape(-1, BLK, head_count * head_width)  9.66 us
    all_gather x1, blocking collectives, body(): lax.all_gather(total_share.astype(jnp.bfloat16), 'dp', axis=0, tiled=True)  8.76 us
    sub x2, other arithmetic, features(): jax.nn.softmax(-logits, axis=-1)  7.99 us
    dot_general x1, matrix products, body(): jnp.einsum('thf,shf->hts', query_feat, key_feat, preferred_element_type=j...  7.41 us
  transfers between devices with their start and end apart: 3, of which 2 were waited for; matrix products, arithmetic and copies ran while one was open for 30% of the time, Pallas kernels for 0%

profile of v1, /device:TPU:0, one launch (start us, length us, event | category | flops | bytes accessed | tf_op | source)
XLA Modules:
  0.0 179.8 jit_solution(11901757053926692517)
XLA Ops:
  8.8 2.4 %fusion.63 = (f32[128,32]{0,1:T(8,128)S(1)}, f32[128,32,128]{0,2,1:T(8,128)}) fusion(bf16[32,128,128]{2,1,0:T(8,128)(2,1)S(1)} %copy-done, bf16[128,32,128]{2,1,0:T(8,128)(2,1)S(1)} %bitcast.136), kind=kOutput, calls=%fused_computation.102 | convolution fusion | flops 135790720 | bytes 4210688 | tf_op jit(solution)/shard_map/sub | solution.py:18
  14.6 2.5 %copy.95 = bf16[16,8,32,128]{3,2,1,0:T(8,128)(2,1)} copy(bf16[16,8,32,128]{3,1,2,0:T(8,128)(2,1)} %bitcast.144) | data formatting | bytes 2097152
  20.8 2.7 %fusion.38 = f32[32,256,128]{2,1,0:T(8,128)} fusion(bf16[128,32,128]{0,2,1:T(8,128)(2,1)S(1)} %get-tuple-element.29, bf16[128,32,128]{0,2,1:T(8,128)(2,1)S(1)} %get-tuple-element.30, pred[128]{0:T(512)(128)(4,1)S(1)} %add_compare_fusion, bf16[128,32,128]{2,1,0:T(8,128)(2,1)S(1)} %bitcast.145), kind=kOutput, calls=%fused_computation.58 | convolution fusion | flops 273678336 | bytes 7340160 | tf_op jit(solution)/shard_map/shf,she->hfe/dot_general | solution.py:60
  26.4 8.9 %all-reduce.4 = (s32[8]{0:T(128)S(1)}, s32[4]{0:T(128)S(1)}) all-reduce(s32[8]{0:T(128)S(1)} %get-tuple-element.8, s32[4]{0:T(128)S(1)} %bitcast_dynamic-update-slice_fusion.1), channel_id=1, replica_groups=mesh['group'=8,'dp'=4] {'dp'}, use_global_device_ids=true, to_apply=%add | all-reduce | flops 12 | bytes 96
  37.4 3.4 %copy.96 = bf16[32,8,32,128]{3,2,1,0:T(8,128)(2,1)} copy(bf16[32,8,32,128]{3,1,2,0:T(8,128)(2,1)} %bitcast.139) | data formatting | bytes 4194304
  47.2 16.8 %all-reduce.5 = (bf16[32,256]{1,0:T(8,128)(2,1)S(1)}, f32[4]{0:T(128)S(1)}) all-reduce(f32[32,256]{1,0:T(8,128)S(1)} %convert_reduce_fusion, f32[4]{0:T(128)S(1)} %bitcast_dynamic-update-slice_fusion), channel_id=3, replica_groups=mesh['group'=8,'dp'=4] {'dp'}, use_global_device_ids=true, to_apply=%region_15.16.clone | all-reduce | flops 8196 | bytes 49184
  64.0 8.8 %all_gather.13 = bf16[32,256]{1,0:T(8,128)(2,1)S(1)} all-gather(bf16[8,256]{1,0:T(8,128)(2,1)S(1)} %dynamic-slice_convert_fusion), channel_id=1, replica_groups=mesh['group'=8,'dp'=4] {'dp'}, dimensions={0}, use_global_device_ids=true | all-gather | bytes 20480 | tf_op jit(solution)/shard_map/all_gather | solution.py:72
  72.9 3.3 %fusion.31 = f32[32,128,256]{2,1,0:T(8,128)S(1)} fusion(bf16[32,128,128]{2,1,0:T(8,128)(2,1)} %param.20, bf16[256,32,128]{2,1,0:T(8,128)(2,1)} %bitcast.135), kind=kOutput, calls=%fused_computation.50 | convolution fusion | flops 268435456 | bytes 7340032 | tf_op jit(solution)/shard_map/thd,hdf->thf/dot_general | solution.py:16
  76.1 4.0 %fusion.61 = (f32[256,32]{0,1:T(8,128)S(1)}, f32[256,32,128]{0,2,1:T(8,128)S(1)}) fusion(f32[32,128,256]{2,1,0:T(8,128)S(1)} %fusion.31), kind=kOutput, calls=%fused_computation.100 | output fusion | flops 4194431 | bytes 8421376 | tf_op jit(solution)/shard_map/sub | solution.py:18
  80.1 3.9 %fusion.62 = (f32[256,32]{0,1:T(8,128)S(1)}, f32[256,32,128]{0,2,1:T(8,128)S(1)}) fusion(f32[32,128,256]{2,1,0:T(8,128)S(1)} %fusion.31), kind=kOutput, calls=%fused_computation.101 | output fusion | flops 2097279 | bytes 8421376 | tf_op jit(solution)/shard_map/sub | solution.py:18
  87.4 4.0 %fusion.59 = (f32[256,32]{0,1:T(8,128)S(1)}, f32[256,32,128]{0,2,1:T(8,128)S(1)}) fusion(f32[32,128,256]{2,1,0:T(8,128)S(1)} %fusion.29), kind=kOutput, calls=%fused_computation.98 | output fusion | flops 4194431 | bytes 8421376 | tf_op jit(solution)/shard_map/sub | solution.py:18
  91.4 3.9 %fusion.60 = (f32[256,32]{0,1:T(8,128)S(1)}, f32[256,32,128]{0,2,1:T(8,128)S(1)}) fusion(f32[32,128,256]{2,1,0:T(8,128)S(1)} %fusion.29), kind=kOutput, calls=%fused_computation.99 | output fusion | flops 2097279 | bytes 8421376 | tf_op jit(solution)/shard_map/sub | solution.py:18
  95.3 3.2 %divide_convert_fusion = (bf16[256,32,128]{0,2,1:T(8,128)(2,1)}, bf16[256,32,128]{0,2,1:T(8,128)(2,1)}) fusion(f32[256,32,128]{0,2,1:T(8,128)S(1)} %get-tuple-element.12, f32[256,32]{0,1:T(8,128)S(1)} %get-tuple-element.11, f32[256,32,128]{0,2,1:T(8,128)S(1)} %get-tuple-element.14, f32[256,32]{0,1:T(8,128)S(1)} %get-tuple-element.13), kind=kLoop, calls=%fused_computation.32 | loop fusion | flops 4194304 | bytes 12648448 | tf_op jit(solution)/shard_map/convert.2
  101.6 3.8 %all-to-all-start = ((bf16[4,8,256,128]{2,3,1,0:T(8,128)(2,1)}), bf16[4,8,256,128]{2,3,1,0:T(8,128)(2,1)S(1)}, u32[]{:S(2)}, u32[]{:S(2)}) async-start(bf16[4,8,256,128]{2,3,1,0:T(8,128)(2,1)} %stack.2), calls=%async_computation.1 | async-start | bytes 4194304 | tf_op jit(solution)/shard_map/all_to_all | solution.py:11
  105.5 7.4 %select_reduce_fusion = (f32[32,256]{1,0:T(8,128)S(1)}, bf16[32,256,256]{1,2,0:T(8,128)(2,1)}) fusion(pred[256,256]{0,1:T(8,128)(4,1)S(1)} %iota_compare_fusion, bf16[256,32,128]{0,2,1:T(8,128)(2,1)} %get-tuple-element.25, bf16[256,32,128]{0,2,1:T(8,128)(2,1)} %get-tuple-element.26, bf16[256,32,128]{0,2,1:T(8,128)(2,1)} %copy-done.7, ...), kind=kOutput, calls=%fused_computation.6 | convolution fusion | flops 1096802304 | bytes 12681216 | tf_op jit(solution)/shard_map/thf,shf->hts/dot_general | solution.py:76
  112.9 5.9 %fusion.6 = f32[32,256,128]{1,2,0:T(8,128)} fusion(bf16[32,256,256]{1,2,0:T(8,128)(2,1)} %get-tuple-element.20, pred[256,256]{0,1:T(8,128)(4,1)S(1)} %iota_compare_fusion, bf16[256,32,128]{2,1,0:T(8,128)(2,1)S(1)} %bitcast.141), kind=kOutput, calls=%fused_computation.10 | convolution fusion | flops 538968064 | bytes 10551296 | tf_op jit(solution)/shard_map/hts,she->the/dot_general | solution.py:79
  118.8 4.6 %all-to-all-done = bf16[4,8,256,128]{2,3,1,0:T(8,128)(2,1)S(1)} async-done(((bf16[4,8,256,128]{2,3,1,0:T(8,128)(2,1)}), bf16[4,8,256,128]{2,3,1,0:T(8,128)(2,1)S(1)}, u32[]{:S(2)}, u32[]{:S(2)}) %all-to-all-start) | async-done | bytes 2097184 | tf_op jit(solution)/shard_map/all_to_all | solution.py:11
  124.8 4.8 %fusion.13 = bf16[256,32,128]{0,2,1:T(8,128)(2,1)S(1)} fusion(f32[32,256,128]{1,2,0:T(8,128)} %fusion.6, f32[256,32]{0,1:T(8,128)S(1)} %add_bitcast_fusion, pred[256]{0:T(512)(128)(4,1)S(1)} %iota_compare_fusion.1, bf16[32,256,128]{1,2,0:T(8,128)(2,1)} %bitcast.142, bf16[256,32,128]{0,2,1:T(8,128)(2,1)} %copy-done.7, bf16[256,32,128]{0,2,1:T(8,128)(2,1)} %copy-done.8), kind=kOutput, calls=%fused_computation.19 | convolution fusion | flops 551550976 | bytes 12615936 | tf_op jit(solution)/shard_map/thf,hfe->the/dot_general | solution.py:23
  129.6 3.3 %reshape.191 = bf16[4,64,4096]{1,0,2:T(4,128)(2,1)} reshape(bf16[256,32,128]{0,2,1:T(8,128)(2,1)S(1)} %fusion.13) | data formatting | bytes 4194304 | tf_op jit(solution)/shard_map/reshape | solution.py:87
  132.9 6.4 %copy.78 = bf16[4,64,4096]{2,0,1:T(4,128)(2,1)S(1)} copy(bf16[4,64,4096]{1,0,2:T(4,128)(2,1)} %reshape.191) | data formatting | bytes 4194304 | tf_op jit(solution)/shard_map/reshape | solution.py:87
  140.5 2.5 %copy.79 = bf16[4,64,4096]{2,1,0:T(8,128)(2,1)} copy(bf16[4,64,4096]{2,0,1:T(4,128)(2,1)S(1)} %convolution_convert_fusion) | data formatting | bytes 4194304 | tf_op jit(solution)/shard_map/convert_element_type | solution.py:104
  143.0 3.6 %all-to-all-start.1 = ((bf16[4,64,4096]{2,1,0:T(8,128)(2,1)}), bf16[4,64,4096]{2,1,0:T(8,128)(2,1)S(1)}, u32[]{:S(2)}, u32[]{:S(2)}) async-start(bf16[4,64,4096]{2,1,0:T(8,128)(2,1)} %copy.79), calls=%async_computation.2 | async-start | bytes 4194304 | tf_op jit(solution)/shard_map/all_to_all | solution.py:105
  148.5 14.8 %psum.7 = f32[]{:T(128)} all-reduce(f32[]{:T(128)} %multiply_reduce_fusion), channel_id=1, replica_groups=mesh['group'=8,'dp'=4] {'group'}, use_global_device_ids=true, to_apply=%region_20.21 | all-reduce | flops 1 | bytes 8 | tf_op jit(solution)/shard_map/psum | solution.py:112
  165.1 4.4 %all-to-all-done.1 = bf16[4,64,4096]{2,1,0:T(8,128)(2,1)S(1)} async-done(((bf16[4,64,4096]{2,1,0:T(8,128)(2,1)}), bf16[4,64,4096]{2,1,0:T(8,128)(2,1)S(1)}, u32[]{:S(2)}, u32[]{:S(2)}) %all-to-all-start.1) | async-done | bytes 2097184 | tf_op jit(solution)/shard_map/all_to_all | solution.py:105
  (66 shorter events, 31.4 us)
Async XLA Ops:
  7.2 1.6 copy-start
  7.2 91.3 %reduce-scatter.2.cloned.1.call-start = ((), (), s32[]{:S(2)}) async-start(), calls=%async_computation.3 | async-start | bytes 5242880 | tf_op jit(solution)/shard_map/reduce_scatter | solution.py:67
  17.1 3.6 %copy-start.9 = (bf16[16,8,32,128]{3,2,1,0:T(8,128)(2,1)S(1)}, bf16[16,8,32,128]{3,2,1,0:T(8,128)(2,1)}, u32[]{:S(2)}) copy-start(bf16[16,8,32,128]{3,2,1,0:T(8,128)(2,1)} %copy.95) | copy-start | bytes 3145732
  19.4 1.0 copy-start.2
  19.4 1.3 copy-start.3
  20.7 3.4 %copy-start.10 = (u32[32]{0:T(128)S(1)}, u32[32]{0:T(128)}, u32[]{:S(2)}) copy-start(u32[32]{0:T(128)} %constant.66) | copy-start | bytes 388
  20.7 5.5 %copy-start.11 = (s32[1,2]{1,0:T(1,128)S(1)}, s32[1,2]{1,0:T(1,128)}, u32[]{:S(2)}) copy-start(s32[1,2]{1,0:T(1,128)} %param.18) | copy-start | bytes 28
  35.2 5.7 %copy-start.4 = (bf16[1,256,4096]{2,1,0:T(8,128)(2,1)S(1)}, bf16[1,256,4096]{2,1,0:T(8,128)(2,1)}, u32[]{:S(2)}) copy-start(bf16[1,256,4096]{2,1,0:T(8,128)(2,1)} %param.13) | copy-start | bytes 6291460
  85.3 2.0 %copy-start.7 = (bf16[256,32,128]{0,2,1:T(8,128)(2,1)}, bf16[256,32,128]{0,2,1:T(8,128)(2,1)S(1)}, u32[]{:S(2)}) copy-start(bf16[256,32,128]{0,2,1:T(8,128)(2,1)S(1)} %get-tuple-element.27) | copy-start | bytes 6291460
  85.3 2.0 %copy-start.8 = (bf16[256,32,128]{0,2,1:T(8,128)(2,1)}, bf16[256,32,128]{0,2,1:T(8,128)(2,1)S(1)}, u32[]{:S(2)}) copy-start(bf16[256,32,128]{0,2,1:T(8,128)(2,1)S(1)} %get-tuple-element.28) | copy-start | bytes 6291460
  101.6 21.8 %all-to-all-start = ((bf16[4,8,256,128]{2,3,1,0:T(8,128)(2,1)}), bf16[4,8,256,128]{2,3,1,0:T(8,128)(2,1)S(1)}, u32[]{:S(2)}, u32[]{:S(2)}) async-start(bf16[4,8,256,128]{2,3,1,0:T(8,128)(2,1)} %stack.2), calls=%async_computation.1 | async-start | bytes 4194304 | tf_op jit(solution)/shard_map/all_to_all | solution.py:11
  105.5 7.4 %copy-start.5 = (bf16[32,8,32,128]{3,2,1,0:T(8,128)(2,1)S(1)}, bf16[32,8,32,128]{3,2,1,0:T(8,128)(2,1)}, u32[]{:S(2)}) copy-start(bf16[32,8,32,128]{3,2,1,0:T(8,128)(2,1)} %copy.98) | copy-start | bytes 6291460
  123.5 1.3 copy-start.6
  143.0 26.4 %all-to-all-start.1 = ((bf16[4,64,4096]{2,1,0:T(8,128)(2,1)}), bf16[4,64,4096]{2,1,0:T(8,128)(2,1)S(1)}, u32[]{:S(2)}, u32[]{:S(2)}) async-start(bf16[4,64,4096]{2,1,0:T(8,128)(2,1)} %copy.79), calls=%async_computation.2 | async-start | bytes 4194304 | tf_op jit(solution)/shard_map/all_to_all | solution.py:105
  146.7 26.3 %copy-start.1 = (bf16[32,128,128]{2,1,0:T(8,128)(2,1)S(1)}, bf16[32,128,128]{2,1,0:T(8,128)(2,1)}, u32[]{:S(2)}) copy-start(bf16[32,128,128]{2,1,0:T(8,128)(2,1)} %param.21) | copy-start | bytes 3145732
Sparse Core Ops, SparseCore 0:
  23.6 56.4 reduce-scatter.1
